TPU v7x, 32 devices: a whole 2x2x4 slice. The times are simulated.
32 devices in a mesh: groups: 2 (over y), space: 4 (over z), chan: 2 (over x), rep: 2 (over core).
Axes of the slice: x: 2, y: 2, z: 4, core: 2. Of those that a mesh axis runs over, the one named last changes fastest.
Arguments:
- volume: bfloat16 [4, 8, 32, 8, 128], P(('groups', 'rep'), 'space', 'chan'), parts along dimension 0, may hold values from -6 to 6
- early_weight: bfloat16 [3, 3, 3, 128, 128], replicated, may hold values from -0.109375 to 0.109375
- late_weight: bfloat16 [3, 3, 3, 128, 512], P(None, None, None, None, 'chan'), may hold values from -0.109375 to 0.109375
- cotangent: bfloat16 [4, 4, 16, 4, 512], P(('groups', 'rep'), 'space', None, None, 'chan'), parts along dimension 0, may hold values from -6 to 6
Outputs:
- grad_early: bfloat16 [6, 3, 3, 128, 128], P('groups'), parts along dimension 0
- grad_late: bfloat16 [6, 3, 3, 128, 512], P('groups', None, None, None, 'chan'), parts along dimension 0
- grad_volume: bfloat16 [4, 8, 32, 8, 128], P(('groups', 'rep'), 'space', 'chan'), parts along dimension 0
There are 2 independent parts, one for each index of `groups`. A program takes and returns all parts, laid end to end along the dimension named above; an argument that names none is the same for every part. Nothing has to cross between parts.
All inputs are finite; a program needn't handle non-finite values.
Results may differ from a plain program's by a relative error of at most 0.0065.
Values may be sent and summed in bfloat16 or wider, within the bound.
No kernel may reach another device: no remote copies, remote signals or barrier semaphores. Data moves between devices by JAX's collectives and lax.ppermute only.
A program may use at most 64 MiB of HBM per device.

v0:
```python
import math
import jax
import jax.numpy as jnp
from jax import lax
from jax.sharding import PartitionSpec as P


def padded_2(block, sides, width):
    for axis, dim in sides:
        count = lax.axis_size(axis)
        forward = [(i, i + 1) for i in range(count - 1)]
        backward = [(target, source) for source, target in forward]
        low = lax.ppermute(
            lax.slice_in_dim(block, block.shape[dim] - width, None, axis=dim), axis, forward
        )
        high = lax.ppermute(lax.slice_in_dim(block, 0, width, axis=dim), axis, backward)
        block = jnp.concatenate([low, block, high], axis=dim)
    return block


def gelu_tanh(value):
    return jax.nn.gelu(value, approximate=True)


def conv_padded(padded, weight):
    depth = padded.shape[1] - 2
    height = padded.shape[2] - 2
    length = padded.shape[3] - 2
    total = None
    for first in range(3):
        for second in range(3):
            for third in range(3):
                window = padded[
                    :, first : first + depth, second : second + height, third : third + length
                ]
                term = jnp.einsum(
                    "sxyzc,co->sxyzo",
                    window,
                    weight[first, second, third],
                    preferred_element_type=jnp.float32,
                )
                total = term if total is None else total + term
    return total


def kernel_grad(padded, delta):
    depth = delta.shape[1]
    height = delta.shape[2]
    length = delta.shape[3]
    planes = []
    for first in range(3):
        for second in range(3):
            for third in range(3):
                window = padded[
                    :, first : first + depth, second : second + height, third : third + length
                ]
                planes.append(
                    jnp.einsum("sxyzc,sxyzo->co", window, delta, preferred_element_type=jnp.float32)
                )
    stacked = jnp.stack(planes, axis=0)
    return stacked.reshape((3, 3, 3) + stacked.shape[1:])


def flipped(weight):
    return jnp.swapaxes(weight[::-1, ::-1, ::-1], 3, 4)


def pad_dims(field, dims):
    widths = [(1, 1) if place in dims else (0, 0) for place in range(field.ndim)]
    return jnp.pad(field, widths)


def pool_cells(field):
    s, x, y, z, c = field.shape
    return jnp.mean(field.reshape(s, x // 2, 2, y // 2, 2, z // 2, 2, c), axis=(2, 4, 6))


def spread_cells(field):
    s, x, y, z, c = field.shape
    wide = jnp.broadcast_to(field[:, :, None, :, None, :, None, :], (s, x, 2, y, 2, z, 2, c))
    return wide.reshape(s, 2 * x, 2 * y, 2 * z, c) * 0.125


def late_layer(joined, late_weight, cotangent):
    rim = padded_2(joined, (("space", 1),), 1)
    late_pad = pad_dims(rim, (2, 3))
    pre_late = conv_padded(late_pad, late_weight)
    delta_late = jax.vjp(gelu_tanh, pre_late)[1](cotangent.astype(jnp.float32))[0].astype(
        jnp.bfloat16
    )
    late_part = kernel_grad(late_pad, delta_late)
    delta_rim = padded_2(delta_late, (("space", 1),), 1)
    back_partial = conv_padded(pad_dims(delta_rim, (2, 3)), flipped(late_weight))
    return (back_partial, late_part)


def per_device(volume, early_weight, late_weight, cotangent):
    count = (
        cotangent.shape[0]
        * lax.axis_size("rep")
        * cotangent.shape[1]
        * lax.axis_size("space")
        * cotangent.shape[2]
        * cotangent.shape[3]
    )
    scale = 1.0 / math.sqrt(count)
    haloed = padded_2(volume, (("space", 1), ("chan", 2)), 1)
    padded_in = pad_dims(haloed, (3,))
    pre_early = conv_padded(padded_in, early_weight)
    pooled = pool_cells(gelu_tanh(pre_early)).astype(jnp.bfloat16)
    joined = lax.all_gather(pooled, "chan", axis=2, tiled=True)
    back_partial, late_part = late_layer(joined, late_weight, cotangent)
    back_rows = lax.psum_scatter(back_partial, "chan", scatter_dimension=2, tiled=True)
    delta_early = jax.vjp(gelu_tanh, pre_early)[1](spread_cells(back_rows))[0].astype(jnp.bfloat16)
    early_part = kernel_grad(padded_in, delta_early)
    delta_halo = padded_2(delta_early, (("space", 1), ("chan", 2)), 1)
    grad_volume = conv_padded(pad_dims(delta_halo, (3,)), flipped(early_weight)).astype(
        jnp.bfloat16
    )
    early_total = lax.psum(early_part, ("space", "chan", "rep"))
    grad_early = (early_total * scale).astype(jnp.bfloat16)
    late_total = lax.psum(late_part, ("space", "rep"))
    grad_late = (late_total * scale).astype(jnp.bfloat16)
    return (grad_early, grad_late, grad_volume)


def solution(mesh):
    return jax.shard_map(
        per_device,
        mesh=mesh,
        in_specs=(
            P(("groups", "rep"), "space", "chan", None, None),
            P(),
            P(None, None, None, None, "chan"),
            P(("groups", "rep"), "space", None, None, "chan"),
        ),
        out_specs=(
            P("groups", None, None, None, None),
            P("groups", None, None, None, "chan"),
            P(("groups", "rep"), "space", "chan", None, None),
        ),
        check_vma=False,
    )
```

profile of v0, /device:TPU:0, one launch (start us, length us, event | category | flops | bytes accessed | tf_op | source)
XLA Modules:
  0.0 279.8 jit_solution(17251219886939649005)
XLA Ops:
  7.2 0.8 fusion.308
  8.0 4.9 %collective-permute-start = (bf16[1,1,16,8,128]{4,3,2,1,0:T(8,128)(2,1)S(1)}, bf16[1,1,16,8,128]{4,3,2,1,0:T(8,128)(2,1)S(1)}, u32[]{:S(2)}, u32[]{:S(2)}) collective-permute-start(bf16[1,1,16,8,128]{4,3,2,1,0:T(8,128)(2,1)S(1)} %get-tuple-element.12), channel_id=1, source_target_pairs={{0,4},{4,8},{8,12},{1,5},{5,9},{9,13},{2,6},{6,10},{10,14},{3,7},{... | collective-permute-start | bytes 98312 | tf_op jit(solution)/shard_map/ppermute | solution.py:13
  12.9 1.4 collective-permute-start.1
  14.4 3.8 %copy.129 = bf16[3,3,3,128,256]{3,4,2,1,0:T(8,128)(2,1)} copy(bf16[3,3,3,128,256]{4,3,2,1,0:T(8,128)(2,1)} %param.6) | data formatting | bytes 3538944 | tf_op args[2]
  18.2 0.6 collective-permute-done.1
  18.9 3.4 %collective-permute-start.2 = (bf16[1,4,1,8,128]{4,3,2,1,0:T(8,128)(2,1)S(1)}, bf16[1,4,1,8,128]{4,3,2,1,0:T(8,128)(2,1)S(1)}, u32[]{:S(2)}, u32[]{:S(2)}) collective-permute-start(bf16[1,4,1,8,128]{4,3,2,1,0:T(8,128)(2,1)S(1)} %get-tuple-element.7), channel_id=1, source_target_pairs={{0,2},{1,3},{4,6},{5,7},{8,10},{9,11},{12,14},{13,15},{16,18},{17,... | collective-permute-start | bytes 24584 | tf_op jit(solution)/shard_map/ppermute | solution.py:13
  22.3 1.4 collective-permute-start.3
  23.7 1.6 reverse_bitcast_fusion
  25.3 1.7 copy.133
  27.0 1.0 collective-permute-done.3
  32.5 4.5 %all-gather = bf16[16,4,128]{2,0,1:T(8,128)(2,1)S(1)} all-gather(bf16[8,4,128]{2,0,1:T(8,128)(2,1)S(1)} %fusion.279), channel_id=2, replica_groups=mesh['groups'=2,'space'=4,'chan'=2,'rep'=2] {'chan'}, dimensions={0}, use_global_device_ids=true | all-gather | bytes 24576 | tf_op jit(solution)/shard_map/all_gather | solution.py:111
  37.0 3.9 %collective-permute-start.4 = (bf16[1,1,16,4,128]{4,2,3,1,0:T(8,128)(2,1)S(1)}, bf16[1,1,16,4,128]{4,2,3,1,0:T(8,128)(2,1)S(1)}, u32[]{:S(2)}, u32[]{:S(2)}) collective-permute-start(bf16[1,1,16,4,128]{4,2,3,1,0:T(8,128)(2,1)S(1)} %bitcast.1506), channel_id=1, source_target_pairs={{0,4},{4,8},{8,12},{1,5},{5,9},{9,13},{2,6},{6,10},{10,14},{3,7},{... | collective-permute-start | bytes 49160 | tf_op jit(solution)/shard_map/ppermute | solution.py:13
  41.0 1.3 collective-permute-start.5
  42.3 1.2 reverse_bitcast_fusion.1
  43.5 3.1 %collective-permute-done.5 = bf16[1,1,16,4,128]{4,2,3,1,0:T(8,128)(2,1)S(1)} collective-permute-done((bf16[1,1,16,4,128]{4,2,3,1,0:T(8,128)(2,1)S(1)}, bf16[1,1,16,4,128]{4,2,3,1,0:T(8,128)(2,1)S(1)}, u32[]{:S(2)}, u32[]{:S(2)}) %collective-permute-start.5) | collective-permute-done | bytes 16416 | tf_op jit(solution)/shard_map/ppermute | solution.py:16
  50.5 3.5 %collective-permute-start.6 = (bf16[1,1,16,4,256]{4,2,3,1,0:T(8,128)(2,1)S(1)}, bf16[1,1,16,4,256]{4,2,3,1,0:T(8,128)(2,1)S(1)}, u32[]{:S(2)}, u32[]{:S(2)}) collective-permute-start(bf16[1,1,16,4,256]{4,2,3,1,0:T(8,128)(2,1)S(1)} %fusion.92), channel_id=1, source_target_pairs={{0,4},{4,8},{8,12},{1,5},{5,9},{9,13},{2,6},{6,10},{10,14},{3,7},{... | collective-permute-start | bytes 98312 | tf_op jit(solution)/shard_map/ppermute | solution.py:13
  54.0 1.3 collective-permute-start.7
  60.1 1.8 copy-done.1
  65.6 0.8 fusion.64
  66.5 0.9 fusion.2
  67.3 10.6 %reduce-scatter.2.cloned.1.call-done = f32[1,1,8,4,128]{4,2,3,1,0:T(8,128)} async-done(((f32[1,1,16,4,128]{4,2,3,1,0:T(8,128)}), f32[1,1,8,4,128]{4,2,3,1,0:T(8,128)}) %reduce-scatter.2.cloned.1.call-update) | async-done | bytes 16400 | tf_op jit(solution)/shard_map/reduce_scatter | solution.py:113
  77.9 0.7 multiply_bitcast_fusion.1
  79.1 0.9 fusion.60
  80.0 0.2 fusion.59
  80.4 0.2 fusion.57
  80.7 0.2 fusion.56
  81.8 0.2 fusion.51
  82.0 0.2 fusion.50
  82.7 0.2 fusion.47
  83.4 0.2 fusion.44
  83.8 0.2 fusion.42
  84.0 0.2 fusion.41
  84.5 0.2 fusion.39
  84.7 0.2 fusion.38
  85.6 1.2 copy-done.4
  87.0 3.4 %collective-permute-start.8 = (bf16[1,1,16,8,128]{4,3,2,1,0:T(8,128)(2,1)S(1)}, bf16[1,1,16,8,128]{4,3,2,1,0:T(8,128)(2,1)S(1)}, u32[]{:S(2)}, u32[]{:S(2)}) collective-permute-start(bf16[1,1,16,8,128]{4,3,2,1,0:T(8,128)(2,1)S(1)} %get-tuple-element.9), channel_id=1, source_target_pairs={{0,4},{4,8},{8,12},{1,5},{5,9},{9,13},{2,6},{6,10},{10,14},{3,7},{... | collective-permute-start | bytes 98312 | tf_op jit(solution)/shard_map/ppermute | solution.py:13
  90.4 1.3 collective-permute-start.9
  91.7 0.9 fusion.1
  92.6 3.8 %collective-permute-done.9 = bf16[1,1,16,8,128]{4,3,2,1,0:T(8,128)(2,1)S(1)} collective-permute-done((bf16[1,1,16,8,128]{4,3,2,1,0:T(8,128)(2,1)S(1)}, bf16[1,1,16,8,128]{4,3,2,1,0:T(8,128)(2,1)S(1)}, u32[]{:S(2)}, u32[]{:S(2)}) %collective-permute-start.9) | collective-permute-done | bytes 32800 | tf_op jit(solution)/shard_map/ppermute | solution.py:16
  96.4 2.7 collective-permute-start.10
  99.1 1.3 collective-permute-start.11
  100.4 0.8 fusion
  101.3 3.4 %collective-permute-done.11 = bf16[1,4,1,8,128]{4,3,2,1,0:T(8,128)(2,1)S(1)} collective-permute-done((bf16[1,4,1,8,128]{4,3,2,1,0:T(8,128)(2,1)S(1)}, bf16[1,4,1,8,128]{4,3,2,1,0:T(8,128)(2,1)S(1)}, u32[]{:S(2)}, u32[]{:S(2)}) %collective-permute-start.11) | collective-permute-done | bytes 8224 | tf_op jit(solution)/shard_map/ppermute | solution.py:16
  109.0 0.8 fusion.34
  109.8 74.2 %all-reduce.7.cloned.1.call-done = f32[3,3,3,128,128]{4,3,2,1,0:T(8,128)} async-done(((f32[3,3,3,128,128]{4,3,2,1,0:T(8,128)}), f32[3,3,3,128,128]{4,3,2,1,0:T(8,128)}) %all-reduce.7.cloned.1.call-update) | async-done | bytes 1769488 | tf_op jit(solution)/shard_map/psum | solution.py:120
  184.0 2.6 multiply_convert_fusion.1
  186.6 83.0 %all-reduce.9.cloned.1.call-done = f32[3,3,3,128,256]{4,3,2,1,0:T(8,128)} async-done(((f32[3,3,3,128,256]{4,3,2,1,0:T(8,128)}), f32[3,3,3,128,256]{4,3,2,1,0:T(8,128)}) %all-reduce.9.cloned.1.call-update) | async-done | bytes 3538960 | tf_op jit(solution)/shard_map/psum | solution.py:122
  269.6 3.7 %multiply_convert_fusion = bf16[3,3,3,128,256]{4,3,2,1,0:T(8,128)(2,1)} fusion(f32[3,3,3,128,256]{4,3,2,1,0:T(8,128)} %all-reduce.9.cloned.1.call-done), kind=kLoop, calls=%fused_computation | loop fusion | flops 1769472 | bytes 5308416 | tf_op jit(solution)/shard_map/convert_element_type | solution.py:123
  (207 shorter events, 24.9 us)
Async XLA Ops:
  7.2 70.8 %reduce-scatter.2.cloned.1.call-start = ((), (), s32[]{:S(2)}) async-start(), calls=%async_computation.1 | async-start | bytes 49152 | tf_op jit(solution)/shard_map/reduce_scatter | solution.py:113
  8.0 10.2 %collective-permute-start = (bf16[1,1,16,8,128]{4,3,2,1,0:T(8,128)(2,1)S(1)}, bf16[1,1,16,8,128]{4,3,2,1,0:T(8,128)(2,1)S(1)}, u32[]{:S(2)}, u32[]{:S(2)}) collective-permute-start(bf16[1,1,16,8,128]{4,3,2,1,0:T(8,128)(2,1)S(1)} %get-tuple-element.12), channel_id=1, source_target_pairs={{0,4},{4,8},{8,12},{1,5},{5,9},{9,13},{2,6},{6,10},{10,14},{3,7},{... | collective-permute-start | bytes 98312 | tf_op jit(solution)/shard_map/ppermute | solution.py:13
  12.9 5.3 %copy-start.3 = (bf16[1,2,16,8,128]{4,3,2,1,0:T(8,128)(2,1)S(1)}, bf16[1,2,16,8,128]{4,3,2,1,0:T(8,128)(2,1)}, u32[]{:S(2)}) copy-start(bf16[1,2,16,8,128]{4,3,2,1,0:T(8,128)(2,1)} %param.4) | copy-start | bytes 196612
  12.9 5.9 %collective-permute-start.1 = (bf16[1,1,16,8,128]{4,3,2,1,0:T(8,128)(2,1)S(1)}, bf16[1,1,16,8,128]{4,3,2,1,0:T(8,128)(2,1)S(1)}, u32[]{:S(2)}, u32[]{:S(2)}) collective-permute-start(bf16[1,1,16,8,128]{4,3,2,1,0:T(8,128)(2,1)S(1)} %get-tuple-element.11), channel_id=1, source_target_pairs={{4,0},{8,4},{12,8},{5,1},{9,5},{13,9},{6,2},{10,6},{14,10},{7,3},{... | collective-permute-start | bytes 98312 | tf_op jit(solution)/shard_map/ppermute | solution.py:16
  18.2 11.2 %copy-start.13 = (bf16[1,1,16,8,128]{4,3,2,1,0:T(8,128)(2,1)}, bf16[1,1,16,8,128]{4,3,2,1,0:T(8,128)(2,1)S(1)}, u32[]{:S(2)}) copy-start(bf16[1,1,16,8,128]{4,3,2,1,0:T(8,128)(2,1)S(1)} %collective-permute-done) | copy-start | bytes 98308
  18.9 13.1 %copy-start.11 = (bf16[1,1,16,8,128]{4,3,2,1,0:T(8,128)(2,1)}, bf16[1,1,16,8,128]{4,3,2,1,0:T(8,128)(2,1)S(1)}, u32[]{:S(2)}) copy-start(bf16[1,1,16,8,128]{4,3,2,1,0:T(8,128)(2,1)S(1)} %collective-permute-done.1) | copy-start | bytes 98308
  18.9 8.1 %collective-permute-start.2 = (bf16[1,4,1,8,128]{4,3,2,1,0:T(8,128)(2,1)S(1)}, bf16[1,4,1,8,128]{4,3,2,1,0:T(8,128)(2,1)S(1)}, u32[]{:S(2)}, u32[]{:S(2)}) collective-permute-start(bf16[1,4,1,8,128]{4,3,2,1,0:T(8,128)(2,1)S(1)} %get-tuple-element.7), channel_id=1, source_target_pairs={{0,2},{1,3},{4,6},{5,7},{8,10},{9,11},{12,14},{13,15},{16,18},{17,... | collective-permute-start | bytes 24584 | tf_op jit(solution)/shard_map/ppermute | solution.py:13
  22.3 3.0 %copy-start.2 = (bf16[3,3,3,128,128]{4,3,2,1,0:T(8,128)(2,1)S(1)}, bf16[3,3,3,128,128]{4,3,2,1,0:T(8,128)(2,1)}, u32[]{:S(2)}) copy-start(bf16[3,3,3,128,128]{4,3,2,1,0:T(8,128)(2,1)} %param.5) | copy-start | bytes 2654212
  22.3 5.7 %collective-permute-start.3 = (bf16[1,4,1,8,128]{4,3,2,1,0:T(8,128)(2,1)S(1)}, bf16[1,4,1,8,128]{4,3,2,1,0:T(8,128)(2,1)S(1)}, u32[]{:S(2)}, u32[]{:S(2)}) collective-permute-start(bf16[1,4,1,8,128]{4,3,2,1,0:T(8,128)(2,1)S(1)} %get-tuple-element.8), channel_id=1, source_target_pairs={{2,0},{3,1},{6,4},{7,5},{10,8},{11,9},{14,12},{15,13},{18,16},{19,... | collective-permute-start | bytes 24584 | tf_op jit(solution)/shard_map/ppermute | solution.py:16
  27.0 4.6 %copy-start.9 = (bf16[1,4,1,8,128]{4,3,2,1,0:T(8,128)(2,1)}, bf16[1,4,1,8,128]{4,3,2,1,0:T(8,128)(2,1)S(1)}, u32[]{:S(2)}) copy-start(bf16[1,4,1,8,128]{4,3,2,1,0:T(8,128)(2,1)S(1)} %collective-permute-done.2) | copy-start | bytes 24580
  28.0 4.3 %copy-start.7 = (bf16[1,4,1,8,128]{4,3,2,1,0:T(8,128)(2,1)}, bf16[1,4,1,8,128]{4,3,2,1,0:T(8,128)(2,1)S(1)}, u32[]{:S(2)}) copy-start(bf16[1,4,1,8,128]{4,3,2,1,0:T(8,128)(2,1)S(1)} %collective-permute-done.3) | copy-start | bytes 24580
  32.5 14.1 %copy-start = (bf16[3,3,3,128,256]{4,3,2,1,0:T(8,128)(2,1)S(1)}, bf16[3,3,3,128,256]{4,3,2,1,0:T(8,128)(2,1)}, u32[]{:S(2)}) copy-start(bf16[3,3,3,128,256]{4,3,2,1,0:T(8,128)(2,1)} %param.6) | copy-start | bytes 5308420
  37.0 6.5 %collective-permute-start.4 = (bf16[1,1,16,4,128]{4,2,3,1,0:T(8,128)(2,1)S(1)}, bf16[1,1,16,4,128]{4,2,3,1,0:T(8,128)(2,1)S(1)}, u32[]{:S(2)}, u32[]{:S(2)}) collective-permute-start(bf16[1,1,16,4,128]{4,2,3,1,0:T(8,128)(2,1)S(1)} %bitcast.1506), channel_id=1, source_target_pairs={{0,4},{4,8},{8,12},{1,5},{5,9},{9,13},{2,6},{6,10},{10,14},{3,7},{... | collective-permute-start | bytes 49160 | tf_op jit(solution)/shard_map/ppermute | solution.py:13
  41.0 5.6 %collective-permute-start.5 = (bf16[1,1,16,4,128]{4,2,3,1,0:T(8,128)(2,1)S(1)}, bf16[1,1,16,4,128]{4,2,3,1,0:T(8,128)(2,1)S(1)}, u32[]{:S(2)}, u32[]{:S(2)}) collective-permute-start(bf16[1,1,16,4,128]{4,2,3,1,0:T(8,128)(2,1)S(1)} %bitcast.1507), channel_id=1, source_target_pairs={{4,0},{8,4},{12,8},{5,1},{9,5},{13,9},{6,2},{10,6},{14,10},{7,3},{... | collective-permute-start | bytes 49160 | tf_op jit(solution)/shard_map/ppermute | solution.py:16
  48.0 2.3 copy-start.15
  50.5 9.6 %collective-permute-start.6 = (bf16[1,1,16,4,256]{4,2,3,1,0:T(8,128)(2,1)S(1)}, bf16[1,1,16,4,256]{4,2,3,1,0:T(8,128)(2,1)S(1)}, u32[]{:S(2)}, u32[]{:S(2)}) collective-permute-start(bf16[1,1,16,4,256]{4,2,3,1,0:T(8,128)(2,1)S(1)} %fusion.92), channel_id=1, source_target_pairs={{0,4},{4,8},{8,12},{1,5},{5,9},{9,13},{2,6},{6,10},{10,14},{3,7},{... | collective-permute-start | bytes 98312 | tf_op jit(solution)/shard_map/ppermute | solution.py:13
  54.0 7.9 %collective-permute-start.7 = (bf16[1,1,16,4,256]{4,2,3,1,0:T(8,128)(2,1)S(1)}, bf16[1,1,16,4,256]{4,2,3,1,0:T(8,128)(2,1)S(1)}, u32[]{:S(2)}, u32[]{:S(2)}) collective-permute-start(bf16[1,1,16,4,256]{4,2,3,1,0:T(8,128)(2,1)S(1)} %fusion.92), channel_id=1, source_target_pairs={{4,0},{8,4},{12,8},{5,1},{9,5},{13,9},{6,2},{10,6},{14,10},{7,3},{... | collective-permute-start | bytes 98312 | tf_op jit(solution)/shard_map/ppermute | solution.py:16
  60.1 1.8 copy-start.1
  66.4 117.6 %all-reduce.7.cloned.1.call-start = ((), (), s32[]{:S(2)}) async-start(), calls=%async_computation.2 | async-start | bytes 3538944 | tf_op jit(solution)/shard_map/psum | solution.py:120
  78.8 6.6 %copy-start.5 = (bf16[2,16,8,128]{3,2,1,0:T(8,128)(2,1)}, bf16[2,16,8,128]{3,2,1,0:T(8,128)(2,1)S(1)}, u32[]{:S(2)}) copy-start(bf16[2,16,8,128]{3,2,1,0:T(8,128)(2,1)S(1)} %fusion.84) | copy-start | bytes 196612
  78.8 1.6 copy-start.14
  80.2 0.9 copy-start.8
  80.9 0.9 copy-start.10
  83.6 0.9 copy-start.12
  85.6 1.2 copy-start.4
  86.8 182.8 %all-reduce.9.cloned.1.call-start = ((), (), s32[]{:S(2)}) async-start(), calls=%async_computation.3 | async-start | bytes 7077888 | tf_op jit(solution)/shard_map/psum | solution.py:122
  87.0 5.6 %collective-permute-start.8 = (bf16[1,1,16,8,128]{4,3,2,1,0:T(8,128)(2,1)S(1)}, bf16[1,1,16,8,128]{4,3,2,1,0:T(8,128)(2,1)S(1)}, u32[]{:S(2)}, u32[]{:S(2)}) collective-permute-start(bf16[1,1,16,8,128]{4,3,2,1,0:T(8,128)(2,1)S(1)} %get-tuple-element.9), channel_id=1, source_target_pairs={{0,4},{4,8},{8,12},{1,5},{5,9},{9,13},{2,6},{6,10},{10,14},{3,7},{... | collective-permute-start | bytes 98312 | tf_op jit(solution)/shard_map/ppermute | solution.py:13
  90.4 6.0 %collective-permute-start.9 = (bf16[1,1,16,8,128]{4,3,2,1,0:T(8,128)(2,1)S(1)}, bf16[1,1,16,8,128]{4,3,2,1,0:T(8,128)(2,1)S(1)}, u32[]{:S(2)}, u32[]{:S(2)}) collective-permute-start(bf16[1,1,16,8,128]{4,3,2,1,0:T(8,128)(2,1)S(1)} %get-tuple-element.10), channel_id=1, source_target_pairs={{4,0},{8,4},{12,8},{5,1},{9,5},{13,9},{6,2},{10,6},{14,10},{7,3},{... | collective-permute-start | bytes 98312 | tf_op jit(solution)/shard_map/ppermute | solution.py:16
  96.4 4.9 %collective-permute-start.10 = (bf16[1,4,1,8,128]{4,3,2,1,0:T(8,128)(2,1)S(1)}, bf16[1,4,1,8,128]{4,3,2,1,0:T(8,128)(2,1)S(1)}, u32[]{:S(2)}, u32[]{:S(2)}) collective-permute-start(bf16[1,4,1,8,128]{4,3,2,1,0:T(8,128)(2,1)S(1)} %get-tuple-element.5), channel_id=1, source_target_pairs={{0,2},{1,3},{4,6},{5,7},{8,10},{9,11},{12,14},{13,15},{16,18},{17,... | collective-permute-start | bytes 24584 | tf_op jit(solution)/shard_map/ppermute | solution.py:13
  99.1 5.5 %collective-permute-start.11 = (bf16[1,4,1,8,128]{4,3,2,1,0:T(8,128)(2,1)S(1)}, bf16[1,4,1,8,128]{4,3,2,1,0:T(8,128)(2,1)S(1)}, u32[]{:S(2)}, u32[]{:S(2)}) collective-permute-start(bf16[1,4,1,8,128]{4,3,2,1,0:T(8,128)(2,1)S(1)} %get-tuple-element.6), channel_id=1, source_target_pairs={{2,0},{3,1},{6,4},{7,5},{10,8},{11,9},{14,12},{15,13},{18,16},{19,... | collective-permute-start | bytes 24584 | tf_op jit(solution)/shard_map/ppermute | solution.py:16
  105.5 1.4 copy-start.6
Sparse Core Ops, SparseCore 0:
  66.6 11.3 reduce-scatter.1
  87.0 96.9 all-reduce.6
  186.5 83.0 all-reduce.8
where the time goes:
time: 281 us; the launch traced here: 280 us
  waiting for transfers between devices  180 us (64%)
  matrix products  31.2 us (11%)
  starting transfers between devices  30 us (11%)
  between operations  14.4 us (5%)
  local copies, waits for them, and re-layouts  12.3 us (4%)
  other arithmetic  7.75 us (3%)
  blocking collectives  4.48 us (2%)
    psum x1, waiting for transfers between devices, per_device(): late_total = lax.psum(late_part, ('space', 'rep'))  83 us
    psum x1, waiting for transfers between devices, per_device(): early_total = lax.psum(early_part, ('space', 'chan', 'rep'))  74.2 us
    ppermute x6, starting transfers between devices, padded_2(): lax.ppermute(lax.slice_in_dim(block, block.shape[dim] - width, None, axis...  21.8 us
    dot_general x108, matrix products, conv_padded(): jnp.einsum('sxyzc,co->sxyzo', window, weight[first, second, third], prefe...  17.4 us
    dot_general x54, matrix products, kernel_grad(): jnp.einsum('sxyzc,sxyzo->co', window, delta, preferred_element_type=jnp.f...  13.9 us
    ppermute x6, waiting for transfers between devices, padded_2(): lax.ppermute(lax.slice_in_dim(block, 0, width, axis=dim), axis, backward)  11.9 us
    reduce_scatter x1, waiting for transfers between devices, per_device(): lax.psum_scatter(back_partial, 'chan', scatter_dimension=2, tiled=True)  10.6 us
    unnamed x36, local copies, waits for them, and re-layouts  8.58 us
  transfers between devices with their start and end apart: 15, of which 8 were waited for; matrix products, arithmetic and copies ran while one was open for 8% of the time, Pallas kernels for 0%

commit v1 on v0

--- a/solution.py
+++ b/solution.py
@@ -119,7 +119,9 @@
     )
     early_total = lax.psum(early_part, ("space", "chan", "rep"))
     grad_early = (early_total * scale).astype(jnp.bfloat16)
-    late_total = lax.psum(late_part, ("space", "rep"))
+    late_total = late_part
+    for mesh_axis in ("rep", "space"):
+        late_total = lax.psum(late_total, mesh_axis)
     grad_late = (late_total * scale).astype(jnp.bfloat16)
     return (grad_early, grad_late, grad_volume)
 

time: 281 us -> 345 us (1.23)
  waiting for transfers between devices: 180 us -> 244 us
    psum x1 -> x2, waiting for transfers between devices: 83 us -> 132 us  [per_device(): late_total = lax.psum(late_total, mesh_axis)]
    psum x1, waiting for transfers between devices: 74.2 us -> 94.1 us  [per_device(): early_total = lax.psum(early_part, ('space', 'chan', 'rep'))]
    ppermute x6, waiting for transfers between devices: 11.9 us -> 7.4 us  [padded_2(): lax.ppermute(lax.slice_in_dim(block, 0, width, axis=dim), axis, backward)]
    unnamed x36 -> x20, local copies, waits for them, and re-layouts: 8.58 us -> 8.54 us
  transfers between devices with their start and end apart: 15 -> 16, of which waited for: 8 -> 7; matrix products, arithmetic and copies ran while one was open for 8% -> 8% of each run, Pallas kernels for 0% -> 0%
where the time goes in v1:
time: 345 us; the launch traced here: 344 us
  waiting for transfers between devices  244 us (71%)
  starting transfers between devices  29.8 us (9%)
  matrix products  29.3 us (8%)
  between operations  16.2 us (5%)
  local copies, waits for them, and re-layouts  12.2 us (4%)
  other arithmetic  7.75 us (2%)
  blocking collectives  4.48 us (1%)
    psum x2, waiting for transfers between devices, per_device(): late_total = lax.psum(late_total, mesh_axis)  132 us
    psum x1, waiting for transfers between devices, per_device(): early_total = lax.psum(early_part, ('space', 'chan', 'rep'))  94.1 us
    ppermute x6, starting transfers between devices, padded_2(): lax.ppermute(lax.slice_in_dim(block, block.shape[dim] - width, None, axis...  21.6 us
    dot_general x108, matrix products, conv_padded(): jnp.einsum('sxyzc,co->sxyzo', window, weight[first, second, third], prefe...  17.4 us
    dot_general x54, matrix products, kernel_grad(): jnp.einsum('sxyzc,sxyzo->co', window, delta, preferred_element_type=jnp.f...  11.9 us
    reduce_scatter x1, waiting for transfers between devices, per_device(): lax.psum_scatter(back_partial, 'chan', scatter_dimension=2, tiled=True)  10.5 us
    unnamed x20, local copies, waits for them, and re-layouts  8.54 us
    ppermute x6, starting transfers between devices, padded_2(): lax.ppermute(lax.slice_in_dim(block, 0, width, axis=dim), axis, backward)  8.02 us
  transfers between devices with their start and end apart: 16, of which 7 were waited for; matrix products, arithmetic and copies ran while one was open for 8% of the time, Pallas kernels for 0%

profile of v1, /device:TPU:0, one launch (start us, length us, event | category | flops | bytes accessed | tf_op | source)
XLA Modules:
  0.0 344.0 jit_solution(1736699580166071902)
XLA Ops:
  8.0 0.8 fusion.308
  8.8 4.9 %collective-permute-start = (bf16[1,1,16,8,128]{4,3,2,1,0:T(8,128)(2,1)S(1)}, bf16[1,1,16,8,128]{4,3,2,1,0:T(8,128)(2,1)S(1)}, u32[]{:S(2)}, u32[]{:S(2)}) collective-permute-start(bf16[1,1,16,8,128]{4,3,2,1,0:T(8,128)(2,1)S(1)} %get-tuple-element.12), channel_id=1, source_target_pairs={{0,4},{4,8},{8,12},{1,5},{5,9},{9,13},{2,6},{6,10},{10,14},{3,7},{... | collective-permute-start | bytes 98312 | tf_op jit(solution)/shard_map/ppermute | solution.py:13
  13.8 1.4 collective-permute-start.1
  15.2 3.8 %copy.129 = bf16[3,3,3,128,256]{3,4,2,1,0:T(8,128)(2,1)} copy(bf16[3,3,3,128,256]{4,3,2,1,0:T(8,128)(2,1)} %param.6) | data formatting | bytes 3538944 | tf_op args[2]
  19.1 0.6 collective-permute-done.1
  19.7 3.4 collective-permute-start.2
  23.1 1.4 collective-permute-start.3
  24.6 1.6 reverse_bitcast_fusion
  26.2 1.7 copy.133
  27.8 1.0 collective-permute-done.3
  33.4 4.5 %all-gather = bf16[16,4,128]{2,0,1:T(8,128)(2,1)S(1)} all-gather(bf16[8,4,128]{2,0,1:T(8,128)(2,1)S(1)} %fusion.279), channel_id=2, replica_groups=mesh['groups'=2,'space'=4,'chan'=2,'rep'=2] {'chan'}, dimensions={0}, use_global_device_ids=true | all-gather | bytes 24576 | tf_op jit(solution)/shard_map/all_gather | solution.py:111
  37.9 3.9 %collective-permute-start.4 = (bf16[1,1,16,4,128]{4,2,3,1,0:T(8,128)(2,1)S(1)}, bf16[1,1,16,4,128]{4,2,3,1,0:T(8,128)(2,1)S(1)}, u32[]{:S(2)}, u32[]{:S(2)}) collective-permute-start(bf16[1,1,16,4,128]{4,2,3,1,0:T(8,128)(2,1)S(1)} %bitcast.1506), channel_id=1, source_target_pairs={{0,4},{4,8},{8,12},{1,5},{5,9},{9,13},{2,6},{6,10},{10,14},{3,7},{... | collective-permute-start | bytes 49160 | tf_op jit(solution)/shard_map/ppermute | solution.py:13
  41.8 1.3 collective-permute-start.5
  43.1 1.3 reverse_bitcast_fusion.1
  44.4 3.1 collective-permute-done.5
  51.3 3.5 %collective-permute-start.6 = (bf16[1,1,16,4,256]{4,2,3,1,0:T(8,128)(2,1)S(1)}, bf16[1,1,16,4,256]{4,2,3,1,0:T(8,128)(2,1)S(1)}, u32[]{:S(2)}, u32[]{:S(2)}) collective-permute-start(bf16[1,1,16,4,256]{4,2,3,1,0:T(8,128)(2,1)S(1)} %fusion.92), channel_id=1, source_target_pairs={{0,4},{4,8},{8,12},{1,5},{5,9},{9,13},{2,6},{6,10},{10,14},{3,7},{... | collective-permute-start | bytes 98312 | tf_op jit(solution)/shard_map/ppermute | solution.py:13
  54.8 1.3 collective-permute-start.7
  61.4 1.8 copy-done.1
  66.9 0.8 fusion.64
  67.7 0.9 fusion
  68.7 10.5 %reduce-scatter.2.cloned.1.call-done = f32[1,1,8,4,128]{4,2,3,1,0:T(8,128)} async-done(((f32[1,1,16,4,128]{4,2,3,1,0:T(8,128)}), f32[1,1,8,4,128]{4,2,3,1,0:T(8,128)}) %reduce-scatter.2.cloned.1.call-update) | async-done | bytes 16400 | tf_op jit(solution)/shard_map/reduce_scatter | solution.py:113
  79.1 0.7 multiply_bitcast_fusion.1
  80.1 3.4 collective-permute-start.8
  83.6 1.3 collective-permute-start.9
  84.9 0.2 fusion.61
  85.1 0.2 fusion.60
  85.3 0.2 fusion.59
  85.5 0.2 fusion.58
  85.8 0.2 fusion.57
  86.0 0.2 fusion.56
  86.4 0.2 fusion.54
  86.7 0.2 fusion.53
  87.1 0.2 fusion.51
  87.3 0.2 fusion.50
  87.5 0.2 fusion.49
  87.8 0.2 fusion.48
  88.4 0.2 fusion.45
  89.1 0.2 fusion.42
  89.8 0.2 fusion.39
  90.7 2.5 collective-permute-start.10
  93.2 1.3 collective-permute-start.11
  94.7 1.2 copy-done.4
  96.0 2.7 collective-permute-done.11
  103.1 0.8 fusion.34
  103.9 94.1 %all-reduce.8.cloned.1.call-done = f32[3,3,3,128,128]{4,3,2,1,0:T(8,128)} async-done(((f32[3,3,3,128,128]{4,3,2,1,0:T(8,128)}), f32[3,3,3,128,128]{4,3,2,1,0:T(8,128)}) %all-reduce.8.cloned.1.call-update) | async-done | bytes 1769488 | tf_op jit(solution)/shard_map/psum | solution.py:120
  198.0 2.6 multiply_convert_fusion.1
  200.6 132.1 %all-reduce.12.cloned.1.call-done = f32[3,3,3,128,256]{4,3,2,1,0:T(8,128)} async-done(((f32[3,3,3,128,256]{4,3,2,1,0:T(8,128)}), f32[3,3,3,128,256]{4,3,2,1,0:T(8,128)}) %all-reduce.12.cloned.1.call-update) | async-done | bytes 3538960 | tf_op jit(solution)/shard_map/psum | solution.py:124
  332.7 3.7 %multiply_convert_fusion = bf16[3,3,3,128,256]{4,3,2,1,0:T(8,128)(2,1)} fusion(f32[3,3,3,128,256]{4,3,2,1,0:T(8,128)} %all-reduce.12.cloned.1.call-done), kind=kLoop, calls=%fused_computation | loop fusion | flops 1769472 | bytes 5308416 | tf_op jit(solution)/shard_map/convert_element_type | solution.py:125
  (194 shorter events, 24.8 us)
Async XLA Ops:
  8.0 71.1 %reduce-scatter.2.cloned.1.call-start = ((), (), s32[]{:S(2)}) async-start(), calls=%async_computation.1 | async-start | bytes 49152 | tf_op jit(solution)/shard_map/reduce_scatter | solution.py:113
  8.8 10.2 %collective-permute-start = (bf16[1,1,16,8,128]{4,3,2,1,0:T(8,128)(2,1)S(1)}, bf16[1,1,16,8,128]{4,3,2,1,0:T(8,128)(2,1)S(1)}, u32[]{:S(2)}, u32[]{:S(2)}) collective-permute-start(bf16[1,1,16,8,128]{4,3,2,1,0:T(8,128)(2,1)S(1)} %get-tuple-element.12), channel_id=1, source_target_pairs={{0,4},{4,8},{8,12},{1,5},{5,9},{9,13},{2,6},{6,10},{10,14},{3,7},{... | collective-permute-start | bytes 98312 | tf_op jit(solution)/shard_map/ppermute | solution.py:13
  13.8 5.3 %copy-start.3 = (bf16[1,2,16,8,128]{4,3,2,1,0:T(8,128)(2,1)S(1)}, bf16[1,2,16,8,128]{4,3,2,1,0:T(8,128)(2,1)}, u32[]{:S(2)}) copy-start(bf16[1,2,16,8,128]{4,3,2,1,0:T(8,128)(2,1)} %param.4) | copy-start | bytes 196612
  13.8 5.9 %collective-permute-start.1 = (bf16[1,1,16,8,128]{4,3,2,1,0:T(8,128)(2,1)S(1)}, bf16[1,1,16,8,128]{4,3,2,1,0:T(8,128)(2,1)S(1)}, u32[]{:S(2)}, u32[]{:S(2)}) collective-permute-start(bf16[1,1,16,8,128]{4,3,2,1,0:T(8,128)(2,1)S(1)} %get-tuple-element.11), channel_id=1, source_target_pairs={{4,0},{8,4},{12,8},{5,1},{9,5},{13,9},{6,2},{10,6},{14,10},{7,3},{... | collective-permute-start | bytes 98312 | tf_op jit(solution)/shard_map/ppermute | solution.py:16
  19.0 11.2 %copy-start.5 = (bf16[1,1,16,8,128]{4,3,2,1,0:T(8,128)(2,1)}, bf16[1,1,16,8,128]{4,3,2,1,0:T(8,128)(2,1)S(1)}, u32[]{:S(2)}) copy-start(bf16[1,1,16,8,128]{4,3,2,1,0:T(8,128)(2,1)S(1)} %collective-permute-done) | copy-start | bytes 98308
  19.7 8.1 %collective-permute-start.2 = (bf16[1,4,1,8,128]{4,3,2,1,0:T(8,128)(2,1)S(1)}, bf16[1,4,1,8,128]{4,3,2,1,0:T(8,128)(2,1)S(1)}, u32[]{:S(2)}, u32[]{:S(2)}) collective-permute-start(bf16[1,4,1,8,128]{4,3,2,1,0:T(8,128)(2,1)S(1)} %get-tuple-element.7), channel_id=1, source_target_pairs={{0,2},{1,3},{4,6},{5,7},{8,10},{9,11},{12,14},{13,15},{16,18},{17,... | collective-permute-start | bytes 24584 | tf_op jit(solution)/shard_map/ppermute | solution.py:13
  23.1 3.0 copy-start.2
  23.1 5.7 %collective-permute-start.3 = (bf16[1,4,1,8,128]{4,3,2,1,0:T(8,128)(2,1)S(1)}, bf16[1,4,1,8,128]{4,3,2,1,0:T(8,128)(2,1)S(1)}, u32[]{:S(2)}, u32[]{:S(2)}) collective-permute-start(bf16[1,4,1,8,128]{4,3,2,1,0:T(8,128)(2,1)S(1)} %get-tuple-element.8), channel_id=1, source_target_pairs={{2,0},{3,1},{6,4},{7,5},{10,8},{11,9},{14,12},{15,13},{18,16},{19,... | collective-permute-start | bytes 24584 | tf_op jit(solution)/shard_map/ppermute | solution.py:16
  33.3 14.1 %copy-start = (bf16[3,3,3,128,256]{4,3,2,1,0:T(8,128)(2,1)S(1)}, bf16[3,3,3,128,256]{4,3,2,1,0:T(8,128)(2,1)}, u32[]{:S(2)}) copy-start(bf16[3,3,3,128,256]{4,3,2,1,0:T(8,128)(2,1)} %param.6) | copy-start | bytes 5308420
  37.9 6.5 %collective-permute-start.4 = (bf16[1,1,16,4,128]{4,2,3,1,0:T(8,128)(2,1)S(1)}, bf16[1,1,16,4,128]{4,2,3,1,0:T(8,128)(2,1)S(1)}, u32[]{:S(2)}, u32[]{:S(2)}) collective-permute-start(bf16[1,1,16,4,128]{4,2,3,1,0:T(8,128)(2,1)S(1)} %bitcast.1506), channel_id=1, source_target_pairs={{0,4},{4,8},{8,12},{1,5},{5,9},{9,13},{2,6},{6,10},{10,14},{3,7},{... | collective-permute-start | bytes 49160 | tf_op jit(solution)/shard_map/ppermute | solution.py:13
  41.8 5.6 %collective-permute-start.5 = (bf16[1,1,16,4,128]{4,2,3,1,0:T(8,128)(2,1)S(1)}, bf16[1,1,16,4,128]{4,2,3,1,0:T(8,128)(2,1)S(1)}, u32[]{:S(2)}, u32[]{:S(2)}) collective-permute-start(bf16[1,1,16,4,128]{4,2,3,1,0:T(8,128)(2,1)S(1)} %bitcast.1507), channel_id=1, source_target_pairs={{4,0},{8,4},{12,8},{5,1},{9,5},{13,9},{6,2},{10,6},{14,10},{7,3},{... | collective-permute-start | bytes 49160 | tf_op jit(solution)/shard_map/ppermute | solution.py:16
  48.9 2.3 copy-start.7
  51.3 10.0 %collective-permute-start.6 = (bf16[1,1,16,4,256]{4,2,3,1,0:T(8,128)(2,1)S(1)}, bf16[1,1,16,4,256]{4,2,3,1,0:T(8,128)(2,1)S(1)}, u32[]{:S(2)}, u32[]{:S(2)}) collective-permute-start(bf16[1,1,16,4,256]{4,2,3,1,0:T(8,128)(2,1)S(1)} %fusion.92), channel_id=1, source_target_pairs={{0,4},{4,8},{8,12},{1,5},{5,9},{9,13},{2,6},{6,10},{10,14},{3,7},{... | collective-permute-start | bytes 98312 | tf_op jit(solution)/shard_map/ppermute | solution.py:13
  54.8 8.3 %collective-permute-start.7 = (bf16[1,1,16,4,256]{4,2,3,1,0:T(8,128)(2,1)S(1)}, bf16[1,1,16,4,256]{4,2,3,1,0:T(8,128)(2,1)S(1)}, u32[]{:S(2)}, u32[]{:S(2)}) collective-permute-start(bf16[1,1,16,4,256]{4,2,3,1,0:T(8,128)(2,1)S(1)} %fusion.92), channel_id=1, source_target_pairs={{4,0},{8,4},{12,8},{5,1},{9,5},{13,9},{6,2},{10,6},{14,10},{7,3},{... | collective-permute-start | bytes 98312 | tf_op jit(solution)/shard_map/ppermute | solution.py:16
  61.3 1.8 copy-start.1
  67.7 33.2 %all-reduce.10.cloned.1.call-start = ((), (), s32[]{:S(2)}) async-start(), calls=%async_computation.3 | async-start | bytes 7077888 | tf_op jit(solution)/shard_map/psum | solution.py:124
  68.6 129.4 %all-reduce.8.cloned.1.call-start = ((), (), s32[]{:S(2)}) async-start(), calls=%async_computation.2 | async-start | bytes 3538944 | tf_op jit(solution)/shard_map/psum | solution.py:120
  80.1 10.5 %collective-permute-start.8 = (bf16[1,1,16,8,128]{4,3,2,1,0:T(8,128)(2,1)S(1)}, bf16[1,1,16,8,128]{4,3,2,1,0:T(8,128)(2,1)S(1)}, u32[]{:S(2)}, u32[]{:S(2)}) collective-permute-start(bf16[1,1,16,8,128]{4,3,2,1,0:T(8,128)(2,1)S(1)} %get-tuple-element.9), channel_id=1, source_target_pairs={{0,4},{4,8},{8,12},{1,5},{5,9},{9,13},{2,6},{6,10},{10,14},{3,7},{... | collective-permute-start | bytes 98312 | tf_op jit(solution)/shard_map/ppermute | solution.py:13
  83.6 2.2 copy-start.6
  83.6 7.1 %collective-permute-start.9 = (bf16[1,1,16,8,128]{4,3,2,1,0:T(8,128)(2,1)S(1)}, bf16[1,1,16,8,128]{4,3,2,1,0:T(8,128)(2,1)S(1)}, u32[]{:S(2)}, u32[]{:S(2)}) collective-permute-start(bf16[1,1,16,8,128]{4,3,2,1,0:T(8,128)(2,1)S(1)} %get-tuple-element.10), channel_id=1, source_target_pairs={{4,0},{8,4},{12,8},{5,1},{9,5},{13,9},{6,2},{10,6},{14,10},{7,3},{... | collective-permute-start | bytes 98312 | tf_op jit(solution)/shard_map/ppermute | solution.py:16
  90.7 5.3 %collective-permute-start.10 = (bf16[1,4,1,8,128]{4,3,2,1,0:T(8,128)(2,1)S(1)}, bf16[1,4,1,8,128]{4,3,2,1,0:T(8,128)(2,1)S(1)}, u32[]{:S(2)}, u32[]{:S(2)}) collective-permute-start(bf16[1,4,1,8,128]{4,3,2,1,0:T(8,128)(2,1)S(1)} %get-tuple-element.5), channel_id=1, source_target_pairs={{0,2},{1,3},{4,6},{5,7},{8,10},{9,11},{12,14},{13,15},{16,18},{17,... | collective-permute-start | bytes 24584 | tf_op jit(solution)/shard_map/ppermute | solution.py:13
  93.2 5.5 %collective-permute-start.11 = (bf16[1,4,1,8,128]{4,3,2,1,0:T(8,128)(2,1)S(1)}, bf16[1,4,1,8,128]{4,3,2,1,0:T(8,128)(2,1)S(1)}, u32[]{:S(2)}, u32[]{:S(2)}) collective-permute-start(bf16[1,4,1,8,128]{4,3,2,1,0:T(8,128)(2,1)S(1)} %get-tuple-element.6), channel_id=1, source_target_pairs={{2,0},{3,1},{6,4},{7,5},{10,8},{11,9},{14,12},{15,13},{18,16},{19,... | collective-permute-start | bytes 24584 | tf_op jit(solution)/shard_map/ppermute | solution.py:16
  94.7 1.2 copy-start.4
  95.9 236.8 %all-reduce.12.cloned.1.call-start = ((), (), s32[]{:S(2)}) async-start(), calls=%async_computation.4 | async-start | bytes 7077888 | tf_op jit(solution)/shard_map/psum | solution.py:124
Sparse Core Ops, SparseCore 0:
  67.8 11.2 reduce-scatter.1
Sparse Core Ops, SparseCore 1:
  70.5 25.3 all-reduce.9
  100.2 97.7 all-reduce.7
  200.2 132.5 all-reduce.11
